TPU v7x, 256 devices: a whole 4x4x8 slice. The times are simulated.
256 devices in a mesh: feat: 32 (over y, z), dp: 8 (over x, core).
Axes of the slice: x: 4, y: 4, z: 8, core: 2. Of those that a mesh axis runs over, the one named last changes fastest.
Arguments:
- face_grid: bfloat16 [32768, 10240], P('dp', 'feat'), may hold values from -6 to 6
- first_nbrs: int32 [16384, 8], P('dp'), may hold values from 0 to 4095
- first_count: int32 [16384], P('dp'), may hold values from 1 to 8
- w_first: bfloat16 [10240, 256], P('feat'), may hold values from -0.0625 to 0.0625
- b_first: float32 [256], replicated, may hold values from -3 to 3
- send_rows: int32 [4096], P('dp'), may hold values from 0 to 2047
- second_nbrs: int32 [16384, 8], P(('dp', 'feat')), may hold values from 0 to 2559
- second_count: int32 [16384], P(('dp', 'feat')), may hold values from 1 to 8
- w_in: bfloat16 [256, 1024], replicated, may hold values from -0.375 to 0.375
- w_out: bfloat16 [1024, 256], replicated, may hold values from -0.1875 to 0.1875
- out_grad: bfloat16 [16384, 256], P(('dp', 'feat')), may hold values from -6 to 6
Outputs:
- embed: bfloat16 [16384, 256], P(('dp', 'feat'))
- grad_first: float32 [10240, 256], P('feat')
Inputs may be any that keep to these rules, and one draw needn't show every extreme that they name: `first_count`: slots at or past a target's count are ignored; counts lie in 1 to 8. `first_nbrs`: only slots below first_count are read. `second_count`: slots at or past a target's count are ignored. `second_nbrs`: indices below 2048 name the partition's own targets, the rest the faces received from the previous partition in order; only slots below second_count are read. `send_rows`: entries may repeat.
All inputs are finite; a program needn't handle non-finite values.
Results may differ from a plain program's by a relative error of at most 0.0061.
Values may be sent and summed in bfloat16 or wider, within the bound.
No kernel may reach another device: no remote copies, remote signals or barrier semaphores. Data moves between devices by JAX's collectives and lax.ppermute only.
A program may use at most 64 MiB of HBM per device.

v0:
```python
import jax
import jax.numpy as jnp
from jax import lax
from jax.sharding import PartitionSpec as P


def passed_along(shard, axis, by):
    devices = lax.axis_size(axis)
    return lax.ppermute(shard, axis, [(i, (i + by) % devices) for i in range(devices)])


def slope(value):
    sig = jax.nn.sigmoid(value)
    return sig * (1.0 + value * (1.0 - sig))


def mean_rows(table, nbrs, count):
    total = jnp.zeros((nbrs.shape[0], table.shape[1]), jnp.float32)
    for slot in range(nbrs.shape[1]):
        picked = table[nbrs[:, slot]].astype(jnp.float32)
        total = total + jnp.where((slot < count)[:, None], picked, 0.0)
    return total / count[:, None].astype(jnp.float32)


def spread(grad, nbrs, count, size):
    slots = jnp.arange(nbrs.shape[1], dtype=jnp.int32)
    factor = jnp.where(
        slots[None, :] < count[:, None], 1.0 / count[:, None].astype(jnp.float32), 0.0
    )
    terms = (grad[:, None, :] * factor[:, :, None]).reshape(-1, grad.shape[1])
    return jax.ops.segment_sum(terms, nbrs.reshape(-1), num_segments=size)


def body(
    face_grid,
    first_nbrs,
    first_count,
    w_first,
    b_first,
    send_rows,
    second_nbrs,
    second_count,
    w_in,
    w_out,
    out_grad,
):
    targets = first_nbrs.shape[0]
    agg_first = (
        face_grid[:targets].astype(jnp.float32) + mean_rows(face_grid, first_nbrs, first_count)
    ).astype(jnp.bfloat16)
    partial_value = jnp.dot(agg_first, w_first, preferred_element_type=jnp.float32)
    pre_own = lax.psum_scatter(partial_value, "feat", scatter_dimension=0, tiled=True) + b_first
    hidden_own = jax.nn.silu(pre_own).astype(jnp.bfloat16)
    table = lax.all_gather(hidden_own, "feat", axis=0, tiled=True)
    received = passed_along(table[send_rows], "dp", 1)
    extended = jnp.concatenate([table, received], axis=0)
    agg_second = (
        hidden_own.astype(jnp.float32) + mean_rows(extended, second_nbrs, second_count)
    ).astype(jnp.bfloat16)
    pre_mlp = jnp.dot(agg_second, w_in, preferred_element_type=jnp.float32)
    act_mlp = jax.nn.silu(pre_mlp).astype(jnp.bfloat16)
    embed = (
        hidden_own.astype(jnp.float32) + jnp.dot(act_mlp, w_out, preferred_element_type=jnp.float32)
    ).astype(jnp.bfloat16)
    grad_act = lax.dot_general(
        out_grad, w_out, (((1,), (1,)), ((), ())), preferred_element_type=jnp.float32
    )
    grad_pre_mlp = (grad_act * slope(pre_mlp)).astype(jnp.bfloat16)
    grad_agg = lax.dot_general(
        grad_pre_mlp, w_in, (((1,), (1,)), ((), ())), preferred_element_type=jnp.float32
    )
    grad_ext = spread(grad_agg, second_nbrs, second_count, extended.shape[0])
    full_rows = table.shape[0]
    returned = passed_along(grad_ext[full_rows:].astype(jnp.bfloat16), "dp", -1).astype(jnp.float32)
    table_grad = grad_ext[:full_rows].at[send_rows].add(returned)
    own_terms = out_grad.astype(jnp.float32) + grad_agg
    grad_own = (
        lax.psum_scatter(
            table_grad.astype(jnp.bfloat16), "feat", scatter_dimension=0, tiled=True
        ).astype(jnp.float32)
        + own_terms
    )
    grad_pre_own = (grad_own * slope(pre_own)).astype(jnp.bfloat16)
    grad_pre_first = lax.all_gather(grad_pre_own, "feat", axis=0, tiled=True)
    slice_grad = lax.dot_general(
        agg_first, grad_pre_first, (((0,), (0,)), ((), ())), preferred_element_type=jnp.float32
    )
    grad_first = lax.psum(slice_grad, "dp")
    return (embed, grad_first)


def solution(mesh):
    return jax.shard_map(
        body,
        mesh=mesh,
        in_specs=(
            P("dp", "feat"),
            P("dp", None),
            P("dp"),
            P("feat", None),
            P(),
            P("dp"),
            P(("dp", "feat"), None),
            P(("dp", "feat")),
            P(),
            P(),
            P(("dp", "feat"), None),
        ),
        out_specs=(P(("dp", "feat"), None), P("feat", None)),
        check_vma=False,
    )
```

profile of v0, /device:TPU:8, one launch (start us, length us, event | category | flops | bytes accessed | tf_op | source)
XLA Modules:
  0.0 828.4 jit_solution(5859287706951482798)
XLA Ops:
  8.7 4.6 copy.22
  13.4 11.2 %gather_fusion = bf16[2048,320]{1,0:T(8,128)(2,1)} fusion(bf16[4096,320]{1,0:T(8,128)(2,1)} %copy.22, s32[2048]{0:T(1024)S(1)} %broadcast_clamp_fusion.7), kind=kCustom, calls=%fused_computation | custom fusion | bytes 2629632 | tf_op jit(solution)/shard_map/gather | solution.py:20
  24.6 11.2 %gather_fusion.1 = bf16[2048,320]{1,0:T(8,128)(2,1)} fusion(bf16[4096,320]{1,0:T(8,128)(2,1)} %copy.22, s32[2048]{0:T(1024)S(1)} %broadcast_clamp_fusion.6), kind=kCustom, calls=%fused_computation.1 | custom fusion | bytes 2629632 | tf_op jit(solution)/shard_map/gather | solution.py:20
  35.8 11.2 %gather_fusion.2 = bf16[2048,320]{1,0:T(8,128)(2,1)} fusion(bf16[4096,320]{1,0:T(8,128)(2,1)} %copy.22, s32[2048]{0:T(1024)S(1)} %broadcast_clamp_fusion.5), kind=kCustom, calls=%fused_computation.2 | custom fusion | bytes 2629632 | tf_op jit(solution)/shard_map/gather | solution.py:20
  47.0 11.2 %gather_fusion.3 = bf16[2048,320]{1,0:T(8,128)(2,1)} fusion(bf16[4096,320]{1,0:T(8,128)(2,1)} %copy.22, s32[2048]{0:T(1024)S(1)} %broadcast_clamp_fusion.4), kind=kCustom, calls=%fused_computation.3 | custom fusion | bytes 2629632 | tf_op jit(solution)/shard_map/gather | solution.py:20
  58.1 11.2 %gather_fusion.4 = bf16[2048,320]{1,0:T(8,128)(2,1)} fusion(bf16[4096,320]{1,0:T(8,128)(2,1)} %copy.22, s32[2048]{0:T(1024)S(1)} %broadcast_clamp_fusion.3), kind=kCustom, calls=%fused_computation.4 | custom fusion | bytes 2629632 | tf_op jit(solution)/shard_map/gather | solution.py:20
  69.3 11.2 %gather_fusion.5 = bf16[2048,320]{1,0:T(8,128)(2,1)} fusion(bf16[4096,320]{1,0:T(8,128)(2,1)} %copy.22, s32[2048]{0:T(1024)S(1)} %broadcast_clamp_fusion.2), kind=kCustom, calls=%fused_computation.5 | custom fusion | bytes 2629632 | tf_op jit(solution)/shard_map/gather | solution.py:20
  80.5 11.2 %gather_fusion.6 = bf16[2048,320]{1,0:T(8,128)(2,1)} fusion(bf16[4096,320]{1,0:T(8,128)(2,1)} %copy.22, s32[2048]{0:T(1024)S(1)} %broadcast_clamp_fusion.1), kind=kCustom, calls=%fused_computation.6 | custom fusion | bytes 2629632 | tf_op jit(solution)/shard_map/gather | solution.py:20
  91.7 11.2 %gather_fusion.7 = bf16[2048,320]{1,0:T(8,128)(2,1)} fusion(bf16[4096,320]{1,0:T(8,128)(2,1)} %copy.22, s32[2048]{0:T(1024)S(1)} %broadcast_clamp_fusion), kind=kCustom, calls=%fused_computation.7 | custom fusion | bytes 2629632 | tf_op jit(solution)/shard_map/gather | solution.py:20
  102.8 8.9 %add_convert_fusion = bf16[2048,320]{1,0:T(8,128)(2,1)S(1)} fusion(bf16[2048,320]{1,0:T(8,128)(2,1)} %gather_fusion.7, bf16[2048,320]{1,0:T(8,128)(2,1)} %gather_fusion.6, bf16[2048,320]{1,0:T(8,128)(2,1)} %gather_fusion.5, bf16[2048,320]{1,0:T(8,128)(2,1)} %gather_fusion.4, bf16[2048,320]{1,0:T(8,128)(2,1)} %gather_fusion.3, ...), kind=kLoop, calls=%fused_computation.19 | loop fusion | flops 17694720 | bytes 13131776 | tf_op jit(solution)/shard_map/convert_element_type | solution.py:50
  113.9 220.8 %reduce-scatter.3.cloned.1.call-done = f32[64,256]{1,0:T(8,128)} async-done(((f32[2048,256]{1,0:T(8,128)}), f32[64,256]{1,0:T(8,128)}) %reduce-scatter.3.cloned.1.call-update) | async-done | bytes 65552 | tf_op jit(solution)/shard_map/reduce_scatter | solution.py:52
  336.6 75.6 %all-gather.3.cloned.1.call-done = bf16[2048,256]{1,0:T(8,128)(2,1)} async-done(((bf16[64,256]{1,0:T(8,128)(2,1)}), bf16[2048,256]{1,0:T(8,128)(2,1)}) %all-gather.3.cloned.1.call-update) | async-done | bytes 1048592 | tf_op jit(solution)/shard_map/all_gather | solution.py:54
  412.2 3.6 gather_fusion.8
  417.3 5.8 collective-permute-done
  426.0 2.2 gather_fusion.11
  428.2 2.1 gather_fusion.12
  441.9 5.1 scatter_custom_fusion
  448.1 3.1 slice.112
  451.9 6.0 scatter_custom_fusion.1
  457.9 2.7 convert_element_type.125
  460.7 215.0 %reduce-scatter.5.cloned.1.call-done = bf16[64,256]{1,0:T(8,128)(2,1)} async-done(((bf16[2048,256]{1,0:T(8,128)(2,1)}), bf16[64,256]{1,0:T(8,128)(2,1)}) %reduce-scatter.5.cloned.1.call-update) | async-done | bytes 32784 | tf_op jit(solution)/shard_map/reduce_scatter | solution.py:78
  677.2 75.9 %all-gather.5.cloned.1.call-done = bf16[2048,256]{1,0:T(8,128)(2,1)} async-done(((bf16[64,256]{1,0:T(8,128)(2,1)}), bf16[2048,256]{1,0:T(8,128)(2,1)}) %all-gather.5.cloned.1.call-update) | async-done | bytes 1048592 | tf_op jit(solution)/shard_map/all_gather | solution.py:84
  753.1 2.5 fusion.41
  756.6 63.6 %all-reduce.2.cloned.1.call-done = f32[320,256]{1,0:T(8,128)} async-done(((f32[320,256]{1,0:T(8,128)}), f32[320,256]{1,0:T(8,128)}) %all-reduce.2.cloned.1.call-update) | async-done | bytes 327696 | tf_op jit(solution)/shard_map/psum | solution.py:88
  (78 shorter events, 27.3 us)
Async XLA Ops:
  7.2 433.9 %copy-start = (bf16[256,1024]{1,0:T(8,128)(2,1)S(1)}, bf16[256,1024]{1,0:T(8,128)(2,1)}, u32[]{:S(2)}) copy-start(bf16[256,1024]{1,0:T(8,128)(2,1)} %param.19) | copy-start | bytes 1572868
  7.2 327.5 %reduce-scatter.3.cloned.1.call-start = ((), (), s32[]{:S(2)}) async-start(), calls=%async_computation.2 | async-start | bytes 2162688 | tf_op jit(solution)/shard_map/reduce_scatter | solution.py:52
  8.7 4.6 copy-start.5
  102.8 8.9 %copy-start.3 = (bf16[320,256]{1,0:T(8,128)(2,1)S(1)}, bf16[320,256]{1,0:T(8,128)(2,1)}, u32[]{:S(2)}) copy-start(bf16[320,256]{1,0:T(8,128)(2,1)} %param.14) | copy-start | bytes 491524
  113.8 220.9 %copy-start.8 = (f32[256]{0:T(256)S(1)}, f32[256]{0:T(256)}, u32[]{:S(2)}) copy-start(f32[256]{0:T(256)} %param.15) | copy-start | bytes 3076
  113.8 222.6 %copy-start.10 = (s32[512]{0:T(512)S(1)}, s32[512]{0:T(512)}, u32[]{:S(2)}) copy-start(s32[512]{0:T(512)} %param.16) | copy-start | bytes 6148
  113.8 222.7 %copy-start.7 = (s32[64,8]{0,1:T(8,128)S(1)}, s32[64,8]{0,1:T(8,128)}, u32[]{:S(2)}) copy-start(s32[64,8]{0,1:T(8,128)} %param.17) | copy-start | bytes 6148
  113.8 222.7 %copy-start.9 = (s32[64]{0:T(128)S(1)}, s32[64]{0:T(128)}, u32[]{:S(2)}) copy-start(s32[64]{0:T(128)} %param.18) | copy-start | bytes 772
  113.8 298.4 %all-gather.3.cloned.1.call-start = ((), (), s32[]{:S(2)}) async-start(), calls=%async_computation.3 | async-start | bytes 1081344 | tf_op jit(solution)/shard_map/all_gather | solution.py:54
  336.2 339.6 %reduce-scatter.5.cloned.1.call-start = ((), (), s32[]{:S(2)}) async-start(), calls=%async_computation.4 | async-start | bytes 1081344 | tf_op jit(solution)/shard_map/reduce_scatter | solution.py:78
  412.2 3.9 copy-start.1
  415.9 7.2 collective-permute-start
  417.3 23.8 %copy-start.4 = (bf16[64,256]{1,0:T(8,128)(2,1)S(1)}, bf16[64,256]{1,0:T(8,128)(2,1)}, u32[]{:S(2)}) copy-start(bf16[64,256]{1,0:T(8,128)(2,1)} %multiply_convert_fusion.3) | copy-start | bytes 98308
  426.0 15.4 %copy-start.6 = (bf16[64,256]{1,0:T(8,128)(2,1)S(1)}, bf16[64,256]{1,0:T(8,128)(2,1)}, u32[]{:S(2)}) copy-start(bf16[64,256]{1,0:T(8,128)(2,1)} %param.21) | copy-start | bytes 98308
  426.0 15.4 %copy-start.11 = (bf16[1024,256]{1,0:T(8,128)(2,1)S(1)}, bf16[1024,256]{1,0:T(8,128)(2,1)}, u32[]{:S(2)}) copy-start(bf16[1024,256]{1,0:T(8,128)(2,1)} %param.20) | copy-start | bytes 1572868
  448.0 3.9 collective-permute-start.1
  457.9 217.8 %copy-start.2 = (f32[64,256]{1,0:T(8,128)S(1)}, f32[64,256]{1,0:T(8,128)}, u32[]{:S(2)}) copy-start(f32[64,256]{1,0:T(8,128)} %reduce-scatter.3.cloned.1.call-done) | copy-start | bytes 196612
  460.7 292.5 %all-gather.5.cloned.1.call-start = ((), (), s32[]{:S(2)}) async-start(), calls=%async_computation.5 | async-start | bytes 1081344 | tf_op jit(solution)/shard_map/all_gather | solution.py:84
  677.2 142.9 %all-reduce.2.cloned.1.call-start = ((), (), s32[]{:S(2)}) async-start(), calls=%async_computation.6 | async-start | bytes 655360 | tf_op jit(solution)/shard_map/psum | solution.py:88
Sparse Core Ops, SparseCore 0:
  113.9 220.6 reduce-scatter.2
  337.8 74.3 all-gather.2
  460.8 214.9 reduce-scatter.4
  678.8 74.3 all-gather.4
  755.9 64.2 all-reduce.1
where the time goes:
time: 830 us; the launch traced here: 828 us
  waiting for transfers between devices  658 us (79%)
  local copies, waits for them, and re-layouts  123 us (15%)
  other arithmetic  27.3 us (3%)
  between operations  14 us (2%)
    reduce_scatter x1, waiting for transfers between devices, body(): lax.psum_scatter(partial_value, 'feat', scatter_dimension=0, tiled=True)  221 us
    reduce_scatter x1, waiting for transfers between devices, body(): lax.psum_scatter(table_grad.astype(jnp.bfloat16), 'feat', scatter_dimensi...  215 us
    gather x16, local copies, waits for them, and re-layouts, mean_rows(): picked = table[nbrs[:, slot]].astype(jnp.float32)  107 us
    all_gather x1, waiting for transfers between devices, body(): grad_pre_first = lax.all_gather(grad_pre_own, 'feat', axis=0, tiled=True)  75.9 us
    all_gather x1, waiting for transfers between devices, body(): table = lax.all_gather(hidden_own, 'feat', axis=0, tiled=True)  75.6 us
    psum x1, waiting for transfers between devices, body(): grad_first = lax.psum(slice_grad, 'dp')  63.6 us
  transfers between devices with their start and end apart: 7, of which 7 were waited for; matrix products, arithmetic and copies ran while one was open for 1% of the time, Pallas kernels for 0%

commit v1 on v0

--- a/solution.py
+++ b/solution.py
@@ -51,7 +51,9 @@
     partial_value = jnp.dot(agg_first, w_first, preferred_element_type=jnp.float32)
     pre_own = lax.psum_scatter(partial_value, "feat", scatter_dimension=0, tiled=True) + b_first
     hidden_own = jax.nn.silu(pre_own).astype(jnp.bfloat16)
-    table = lax.all_gather(hidden_own, "feat", axis=0, tiled=True)
+    table = jnp.concatenate(
+        lax.all_to_all(jnp.stack([hidden_own] * lax.axis_size("feat")), "feat", 0, 0), axis=0
+    )
     received = passed_along(table[send_rows], "dp", 1)
     extended = jnp.concatenate([table, received], axis=0)
     agg_second = (

time: 830 us -> 784 us (0.945)
  waiting for transfers between devices: 658 us -> 600 us
    all_gather x1 -> x0, waiting for transfers between devices: 75.6 us -> none  [body(): table = lax.all_gather(hidden_own, 'feat', axis=0, tiled=True)]
    all_to_all x0 -> x1, waiting for transfers between devices: none -> 19.3 us  [body(): lax.all_to_all(jnp.stack([hidden_own] * lax.axis_size('feat')), 'feat', 0...]
where the time goes in v1:
time: 784 us; the launch traced here: 783 us
  waiting for transfers between devices  600 us (77%)
  local copies, waits for them, and re-layouts  121 us (15%)
  other arithmetic  30.9 us (4%)
  between operations  14 us (2%)
  starting transfers between devices  8.4 us (1%)
  matrix products  8.15 us (1%)
    reduce_scatter x1, waiting for transfers between devices, body(): lax.psum_scatter(partial_value, 'feat', scatter_dimension=0, tiled=True)  221 us
    reduce_scatter x1, waiting for transfers between devices, body(): lax.psum_scatter(table_grad.astype(jnp.bfloat16), 'feat', scatter_dimensi...  215 us
    gather x16, local copies, waits for them, and re-layouts, mean_rows(): picked = table[nbrs[:, slot]].astype(jnp.float32)  106 us
    all_gather x1, waiting for transfers between devices, body(): grad_pre_first = lax.all_gather(grad_pre_own, 'feat', axis=0, tiled=True)  76.1 us
    psum x1, waiting for transfers between devices, body(): grad_first = lax.psum(slice_grad, 'dp')  63.6 us
    all_to_all x1, waiting for transfers between devices, body(): lax.all_to_all(jnp.stack([hidden_own] * lax.axis_size('feat')), 'feat', 0...  19.3 us
  transfers between devices with their start and end apart: 7, of which 7 were waited for; matrix products, arithmetic and copies ran while one was open for 1% of the time, Pallas kernels for 0%

profile of v1, /device:TPU:8, one launch (start us, length us, event | category | flops | bytes accessed | tf_op | source)
XLA Modules:
  0.0 783.0 jit_solution(17550370614504803622)
XLA Ops:
  8.7 4.6 copy.22
  13.4 11.2 %gather_fusion = bf16[2048,320]{1,0:T(8,128)(2,1)} fusion(bf16[4096,320]{1,0:T(8,128)(2,1)} %copy.22, s32[2048]{0:T(1024)S(1)} %broadcast_clamp_fusion.7), kind=kCustom, calls=%fused_computation | custom fusion | bytes 2629632 | tf_op jit(solution)/shard_map/gather | solution.py:20
  24.5 11.2 %gather_fusion.1 = bf16[2048,320]{1,0:T(8,128)(2,1)} fusion(bf16[4096,320]{1,0:T(8,128)(2,1)} %copy.22, s32[2048]{0:T(1024)S(1)} %broadcast_clamp_fusion.6), kind=kCustom, calls=%fused_computation.1 | custom fusion | bytes 2629632 | tf_op jit(solution)/shard_map/gather | solution.py:20
  35.7 11.1 %gather_fusion.2 = bf16[2048,320]{1,0:T(8,128)(2,1)} fusion(bf16[4096,320]{1,0:T(8,128)(2,1)} %copy.22, s32[2048]{0:T(1024)S(1)} %broadcast_clamp_fusion.5), kind=kCustom, calls=%fused_computation.2 | custom fusion | bytes 2629632 | tf_op jit(solution)/shard_map/gather | solution.py:20
  46.8 11.1 %gather_fusion.3 = bf16[2048,320]{1,0:T(8,128)(2,1)} fusion(bf16[4096,320]{1,0:T(8,128)(2,1)} %copy.22, s32[2048]{0:T(1024)S(1)} %broadcast_clamp_fusion.4), kind=kCustom, calls=%fused_computation.3 | custom fusion | bytes 2629632 | tf_op jit(solution)/shard_map/gather | solution.py:20
  58.0 11.1 %gather_fusion.4 = bf16[2048,320]{1,0:T(8,128)(2,1)} fusion(bf16[4096,320]{1,0:T(8,128)(2,1)} %copy.22, s32[2048]{0:T(1024)S(1)} %broadcast_clamp_fusion.3), kind=kCustom, calls=%fused_computation.4 | custom fusion | bytes 2629632 | tf_op jit(solution)/shard_map/gather | solution.py:20
  69.1 11.2 %gather_fusion.5 = bf16[2048,320]{1,0:T(8,128)(2,1)} fusion(bf16[4096,320]{1,0:T(8,128)(2,1)} %copy.22, s32[2048]{0:T(1024)S(1)} %broadcast_clamp_fusion.2), kind=kCustom, calls=%fused_computation.5 | custom fusion | bytes 2629632 | tf_op jit(solution)/shard_map/gather | solution.py:20
  80.3 11.2 %gather_fusion.6 = bf16[2048,320]{1,0:T(8,128)(2,1)} fusion(bf16[4096,320]{1,0:T(8,128)(2,1)} %copy.22, s32[2048]{0:T(1024)S(1)} %broadcast_clamp_fusion.1), kind=kCustom, calls=%fused_computation.6 | custom fusion | bytes 2629632 | tf_op jit(solution)/shard_map/gather | solution.py:20
  91.4 11.2 %gather_fusion.7 = bf16[2048,320]{1,0:T(8,128)(2,1)} fusion(bf16[4096,320]{1,0:T(8,128)(2,1)} %copy.22, s32[2048]{0:T(1024)S(1)} %broadcast_clamp_fusion), kind=kCustom, calls=%fused_computation.7 | custom fusion | bytes 2629632 | tf_op jit(solution)/shard_map/gather | solution.py:20
  102.6 8.9 %add_convert_fusion = bf16[2048,320]{1,0:T(8,128)(2,1)S(1)} fusion(bf16[2048,320]{1,0:T(8,128)(2,1)} %gather_fusion.7, bf16[2048,320]{1,0:T(8,128)(2,1)} %gather_fusion.6, bf16[2048,320]{1,0:T(8,128)(2,1)} %gather_fusion.5, bf16[2048,320]{1,0:T(8,128)(2,1)} %gather_fusion.4, bf16[2048,320]{1,0:T(8,128)(2,1)} %gather_fusion.3, ...), kind=kLoop, calls=%fused_computation.19 | loop fusion | flops 17694720 | bytes 13131776 | tf_op jit(solution)/shard_map/convert_element_type | solution.py:50
  113.6 220.8 %reduce-scatter.3.cloned.1.call-done = f32[64,256]{1,0:T(8,128)} async-done(((f32[2048,256]{1,0:T(8,128)}), f32[64,256]{1,0:T(8,128)}) %reduce-scatter.3.cloned.1.call-update) | async-done | bytes 65552 | tf_op jit(solution)/shard_map/reduce_scatter | solution.py:52
  336.4 8.0 %all-to-all-start = ((bf16[32,64,256]{2,1,0:T(8,128)(2,1)}), bf16[32,64,256]{2,1,0:T(8,128)(2,1)S(1)}, u32[]{:S(2)}, u32[]{:S(2)}) async-start(bf16[32,64,256]{2,1,0:T(8,128)(2,1)} %stack.2), calls=%async_computation.1 | async-start | bytes 2097152 | tf_op jit(solution)/shard_map/all_to_all | solution.py:55
  346.0 19.3 %all-to-all-done = bf16[32,64,256]{2,1,0:T(8,128)(2,1)S(1)} async-done(((bf16[32,64,256]{2,1,0:T(8,128)(2,1)}), bf16[32,64,256]{2,1,0:T(8,128)(2,1)S(1)}, u32[]{:S(2)}, u32[]{:S(2)}) %all-to-all-start) | async-done | bytes 1048608 | tf_op jit(solution)/shard_map/all_to_all | solution.py:55
  370.5 4.5 collective-permute-done
  380.8 2.7 gather_fusion.12
  383.5 2.9 gather_fusion.13
  386.4 2.9 gather_fusion.14
  396.2 5.2 scatter_custom_fusion
  402.5 3.1 slice.112
  406.3 6.0 scatter_custom_fusion.1
  412.3 2.7 convert_element_type.125
  415.1 215.0 %reduce-scatter.5.cloned.1.call-done = bf16[64,256]{1,0:T(8,128)(2,1)} async-done(((bf16[2048,256]{1,0:T(8,128)(2,1)}), bf16[64,256]{1,0:T(8,128)(2,1)}) %reduce-scatter.5.cloned.1.call-update) | async-done | bytes 32784 | tf_op jit(solution)/shard_map/reduce_scatter | solution.py:80
  631.6 76.1 %all-gather.2.cloned.1.call-done = bf16[2048,256]{1,0:T(8,128)(2,1)} async-done(((bf16[64,256]{1,0:T(8,128)(2,1)}), bf16[2048,256]{1,0:T(8,128)(2,1)}) %all-gather.2.cloned.1.call-update) | async-done | bytes 1048592 | tf_op jit(solution)/shard_map/all_gather | solution.py:86
  711.1 63.6 %all-reduce.2.cloned.1.call-done = f32[320,256]{1,0:T(8,128)} async-done(((f32[320,256]{1,0:T(8,128)}), f32[320,256]{1,0:T(8,128)}) %all-reduce.2.cloned.1.call-update) | async-done | bytes 327696 | tf_op jit(solution)/shard_map/psum | solution.py:90
  (77 shorter events, 33.6 us)
Async XLA Ops:
  7.2 386.3 %copy-start = (bf16[256,1024]{1,0:T(8,128)(2,1)S(1)}, bf16[256,1024]{1,0:T(8,128)(2,1)}, u32[]{:S(2)}) copy-start(bf16[256,1024]{1,0:T(8,128)(2,1)} %param.19) | copy-start | bytes 1572868
  7.2 327.2 %reduce-scatter.3.cloned.1.call-start = ((), (), s32[]{:S(2)}) async-start(), calls=%async_computation.3 | async-start | bytes 2162688 | tf_op jit(solution)/shard_map/reduce_scatter | solution.py:52
  8.7 4.6 copy-start.4
  102.6 8.9 %copy-start.3 = (bf16[320,256]{1,0:T(8,128)(2,1)S(1)}, bf16[320,256]{1,0:T(8,128)(2,1)}, u32[]{:S(2)}) copy-start(bf16[320,256]{1,0:T(8,128)(2,1)} %param.14) | copy-start | bytes 491524
  113.5 220.9 %copy-start.7 = (f32[256]{0:T(256)S(1)}, f32[256]{0:T(256)}, u32[]{:S(2)}) copy-start(f32[256]{0:T(256)} %param.15) | copy-start | bytes 3076
  335.3 9.4 %copy-start.10 = (s32[512]{0:T(512)S(1)}, s32[512]{0:T(512)}, u32[]{:S(2)}) copy-start(s32[512]{0:T(512)} %param.16) | copy-start | bytes 6148
  335.3 9.4 %copy-start.6 = (s32[64,8]{0,1:T(8,128)S(1)}, s32[64,8]{0,1:T(8,128)}, u32[]{:S(2)}) copy-start(s32[64,8]{0,1:T(8,128)} %param.17) | copy-start | bytes 6148
  335.3 10.7 %copy-start.9 = (s32[64]{0:T(128)S(1)}, s32[64]{0:T(128)}, u32[]{:S(2)}) copy-start(s32[64]{0:T(128)} %param.18) | copy-start | bytes 772
  336.4 28.9 %all-to-all-start = ((bf16[32,64,256]{2,1,0:T(8,128)(2,1)}), bf16[32,64,256]{2,1,0:T(8,128)(2,1)S(1)}, u32[]{:S(2)}, u32[]{:S(2)}) async-start(bf16[32,64,256]{2,1,0:T(8,128)(2,1)} %stack.2), calls=%async_computation.1 | async-start | bytes 2097152 | tf_op jit(solution)/shard_map/all_to_all | solution.py:55
  344.5 285.7 %reduce-scatter.5.cloned.1.call-start = ((), (), s32[]{:S(2)}) async-start(), calls=%async_computation.4 | async-start | bytes 1081344 | tf_op jit(solution)/shard_map/reduce_scatter | solution.py:80
  367.9 7.2 collective-permute-start
  376.3 13.0 %copy-start.1 = (bf16[2560,256]{1,0:T(8,128)(2,1)S(1)}, bf16[2560,256]{1,0:T(8,128)(2,1)}, u32[]{:S(2)}) copy-start(bf16[2560,256]{1,0:T(8,128)(2,1)} %pad_maximum_fusion) | copy-start | bytes 3932164
  378.5 16.1 %copy-start.5 = (bf16[64,256]{1,0:T(8,128)(2,1)S(1)}, bf16[64,256]{1,0:T(8,128)(2,1)}, u32[]{:S(2)}) copy-start(bf16[64,256]{1,0:T(8,128)(2,1)} %param.21) | copy-start | bytes 98308
  402.4 3.9 collective-permute-start.1
  412.3 217.8 %copy-start.2 = (f32[64,256]{1,0:T(8,128)S(1)}, f32[64,256]{1,0:T(8,128)}, u32[]{:S(2)}) copy-start(f32[64,256]{1,0:T(8,128)} %reduce-scatter.3.cloned.1.call-done) | copy-start | bytes 196612
  412.3 217.8 %copy-start.8 = (f32[256]{0:T(256)S(1)}, f32[256]{0:T(256)}, u32[]{:S(2)}) copy-start(f32[256]{0:T(256)} %param.15) | copy-start | bytes 3076
  415.0 292.7 %all-gather.2.cloned.1.call-start = ((), (), s32[]{:S(2)}) async-start(), calls=%async_computation.5 | async-start | bytes 1081344 | tf_op jit(solution)/shard_map/all_gather | solution.py:86
  631.6 78.7 %copy-start.11 = (bf16[1024,256]{1,0:T(8,128)(2,1)S(1)}, bf16[1024,256]{1,0:T(8,128)(2,1)}, u32[]{:S(2)}) copy-start(bf16[1024,256]{1,0:T(8,128)(2,1)} %param.20) | copy-start | bytes 1572868
  631.6 143.1 %all-reduce.2.cloned.1.call-start = ((), (), s32[]{:S(2)}) async-start(), calls=%async_computation.6 | async-start | bytes 655360 | tf_op jit(solution)/shard_map/psum | solution.py:90
Sparse Core Ops, SparseCore 0:
  113.7 220.6 reduce-scatter.2
  415.2 214.9 reduce-scatter.4
  633.3 74.3 all-gather.1
  710.4 64.2 all-reduce.1
